TPU v7x, 128 devices: a whole 4x4x4 slice. The times are simulated.
128 devices in a mesh: dp: 16 (over z, x_lo, core), space: 8 (over x_hi, y).
Axes of the slice: x: 4 (x_hi: 2, x_lo: 2; x = x_hi * 2 + x_lo), y: 4, z: 4, core: 2. Of those that a mesh axis runs over, the one named last changes fastest.
Arguments:
- features: bfloat16 [16, 128, 64, 1024], P('dp', 'space'), may hold values from -6 to 6
- target: bfloat16 [16, 128, 64, 1024], P('dp', 'space'), may hold values from -6 to 6
- anchors: int32 [16, 2], P('dp'), may hold values from 0 to 64512
- w_first: bfloat16 [3, 3, 64, 64], replicated, may hold values from -0.25 to 0.25
- b_first: float32 [64], replicated, may hold values from -3 to 3
- w_second: bfloat16 [3, 3, 64, 64], replicated, may hold values from -0.25 to 0.25
- b_second: float32 [64], replicated, may hold values from -3 to 3
Outputs:
- back_input: bfloat16 [16, 128, 64, 1024], P('dp', 'space')
- grad_w1: float32 [3, 3, 64, 64], replicated
- grad_b1: float32 [64], replicated
- grad_w2: float32 [3, 3, 64, 64], replicated
- grad_b2: float32 [64], replicated
All inputs are finite; a program needn't handle non-finite values.
Results may differ from a plain program's by a relative error of at most 0.0075.
Values may be sent and summed in bfloat16 or wider, within the bound.
No kernel may reach another device: no remote copies, remote signals or barrier semaphores. Data moves between devices by JAX's collectives and lax.ppermute only.
A program may use at most 128 MiB of HBM per device.

v0:
```python
import math
import jax
import jax.numpy as jnp
from jax import lax
from jax.sharding import PartitionSpec as P


def extended(value, sides, width):
    for axis, dim in sides:
        size, length = (lax.axis_size(axis), value.shape[dim])
        up = [(i, (i + 1) % size) for i in range(size - 1)]
        down = [(j, i) for i, j in up]
        last = lax.slice_in_dim(value, length - width, length, axis=dim)
        first = lax.slice_in_dim(value, 0, width, axis=dim)
        before = lax.ppermute(last, axis, up)
        after = lax.ppermute(first, axis, down)
        value = jnp.concatenate([before, value, after], axis=dim)
    return value


def shift_cols(tensor, offset):
    if offset == 0:
        return tensor
    filler = jnp.zeros(tensor.shape[:-1] + (1,), tensor.dtype)
    if offset > 0:
        return jnp.concatenate([tensor[..., 1:], filler], axis=-1)
    return jnp.concatenate([filler, tensor[..., :-1]], axis=-1)


def unfold(padded):
    inner = padded.shape[1] - 2
    pieces = [
        shift_cols(padded[:, row_off : row_off + inner], col_off - 1)
        for row_off in range(3)
        for col_off in range(3)
    ]
    return jnp.concatenate(pieces, axis=2)


def unfold_back(padded):
    inner = padded.shape[1] - 2
    pieces = [
        shift_cols(padded[:, 2 - row_off : 2 - row_off + inner], 1 - col_off)
        for row_off in range(3)
        for col_off in range(3)
    ]
    return jnp.concatenate(pieces, axis=2)


def forward_matrix(kernel):
    return jnp.transpose(kernel, (2, 0, 1, 3)).reshape(kernel.shape[2], -1)


def backward_matrix(kernel):
    return jnp.transpose(kernel, (3, 0, 1, 2)).reshape(kernel.shape[3], -1)


def fold_kernel(matrix):
    channels = matrix.shape[0]
    return jnp.transpose(matrix.reshape(channels, 3, 3, -1), (1, 2, 0, 3))


def coords(anchor_rows, row_ids, columns, channels):
    chan_ids = jnp.arange(channels, dtype=jnp.int32)
    periods = 4 * jnp.left_shift(jnp.ones_like(chan_ids), chan_ids % 8)
    scaled = 2.0 * math.pi / periods.astype(jnp.float32)
    row_pos = anchor_rows[:, 0][:, None, None] + row_ids[None, :, None]
    row_wave = jnp.sin(
        (row_pos % periods[None, None, :]).astype(jnp.float32) * scaled[None, None, :]
    )
    col_ids = jnp.arange(columns, dtype=jnp.int32)
    col_pos = anchor_rows[:, 1][:, None, None] + col_ids[None, None, :]
    col_wave = jnp.sin(
        (col_pos % periods[None, :, None]).astype(jnp.float32) * scaled[None, :, None]
    )
    use_rows = (chan_ids < channels // 2)[None, None, :, None]
    return jnp.where(use_rows, row_wave[..., None], col_wave[:, None])


def gelu_grad(pre_act, upstream):
    return jax.vjp(lambda inputs: jax.nn.gelu(inputs, approximate=True), pre_act)[1](upstream)[0]


def mixing(form, left, right):
    return jnp.einsum(form, left, right, preferred_element_type=jnp.float32)


def combine(pairs):
    flat_grads = jnp.concatenate([piece.reshape(-1) for pair in pairs for piece in pair])
    total = lax.psum(flat_grads, ("dp", "space"))
    results = []
    start = 0
    for pair in pairs:
        for piece in pair:
            count = piece.size
            results.append(total[start : start + count].reshape(piece.shape))
            start = start + count
    return results


def shards(features, target, anchors, w_first, b_first, w_second, b_second):
    strip_rows = features.shape[1]
    columns = features.shape[3]
    channels = features.shape[2]
    dev_index = lax.axis_index("space")
    crop_rows = strip_rows * lax.axis_size("space")
    factor = 1.0 / math.sqrt(features.shape[0] * lax.axis_size("dp") * crop_rows * columns)
    row_ids = dev_index * strip_rows + jnp.arange(strip_rows, dtype=jnp.int32)
    geo = coords(anchors, row_ids, columns, channels)
    first = (features.astype(jnp.float32) + geo).astype(jnp.bfloat16)
    bias_one = b_first[None, None, :, None]
    first_pad = extended(first, (("space", 1),), 1)
    pre_act = mixing("dk,brkw->brdw", forward_matrix(w_first), unfold(first_pad)) + bias_one
    hidden = jax.nn.gelu(pre_act, approximate=True).astype(jnp.bfloat16)
    hidden_pad = extended(hidden, (("space", 1),), 1)
    output = (
        mixing("dk,brkw->brdw", forward_matrix(w_second), unfold(hidden_pad))
        + b_second[None, None, :, None]
    )
    misfit = (output - target.astype(jnp.float32)).astype(jnp.bfloat16)
    grad_w2 = fold_kernel(mixing("brdw,brkw->dk", misfit, unfold(hidden_pad))) * factor
    grad_b2 = jnp.sum(misfit.astype(jnp.float32), axis=(0, 1, 3)) * factor
    misfit_pad = extended(misfit, (("space", 1),), 1)
    back_hidden = mixing("ck,brkw->brcw", backward_matrix(w_second), unfold_back(misfit_pad))
    slope = gelu_grad(pre_act, back_hidden).astype(jnp.bfloat16)
    grad_w1 = fold_kernel(mixing("brdw,brkw->dk", slope, unfold(first_pad))) * factor
    grad_b1 = jnp.sum(slope.astype(jnp.float32), axis=(0, 1, 3)) * factor
    slope_pad = extended(slope, (("space", 1),), 1)
    back_input = mixing("ck,brkw->brcw", backward_matrix(w_first), unfold_back(slope_pad)).astype(
        jnp.bfloat16
    )
    grad_w2, grad_b2, grad_w1, grad_b1 = combine([(grad_w2, grad_b2), (grad_w1, grad_b1)])
    return (back_input, grad_w1, grad_b1, grad_w2, grad_b2)


def solution(mesh):
    in_specs = (
        P("dp", "space", None, None),
        P("dp", "space", None, None),
        P("dp", None),
        P(),
        P(),
        P(),
        P(),
    )
    out_specs = (P("dp", "space", None, None), P(), P(), P(), P())
    return jax.shard_map(shards, mesh=mesh, in_specs=in_specs, out_specs=out_specs, check_vma=False)
```

profile of v0, /device:TPU:1, one launch (start us, length us, event | category | flops | bytes accessed | tf_op | source)
XLA Modules:
  0.0 301.8 jit_solution(5083959459954517360)
XLA Ops:
  7.3 1.3 fusion.122
  8.6 0.6 iota_add_fusion
  9.2 0.7 add_add_fusion
  9.9 0.2 fusion.111
  10.2 3.5 %fusion.106 = f32[64,1024]{1,0:T(8,128)S(1)} fusion(f32[64]{0:T(128)S(1)} %convert_divide_fusion, s32[64]{0:T(128)S(1)} %compare_select_fusion, s32[1024]{0:T(1024)S(1)} %iota_add_fusion, pred[64]{0:T(512)(128)(4,1)S(1)} %broadcast_compare_fusion), kind=kLoop, calls=%fused_computation.138 | loop fusion | flops 589824 | bytes 266816 | tf_op jit(solution)/shard_map/sin | solution.py:73
  13.6 2.1 add_convert_fusion
  15.8 1.3 collective-permute-start.1
  17.1 4.8 %collective-permute-start = (bf16[1,1,64,1024]{3,2,1,0:T(8,128)(2,1)S(1)}, bf16[1,1,64,1024]{3,2,1,0:T(8,128)(2,1)S(1)}, u32[]{:S(2)}, u32[]{:S(2)}) collective-permute-start(bf16[1,1,64,1024]{3,2,1,0:T(8,128)(2,1)S(1)} %get-tuple-element.28), channel_id=1, source_target_pairs={{0,1},{1,2},{2,3},{3,4},{4,5},{5,6},{6,7},{8,9},{9,10},{10,11},{11... | collective-permute-start | bytes 393224 | tf_op jit(solution)/shard_map/ppermute | solution.py:15
  22.1 0.6 collective-permute-done.1
  22.7 1.0 collective-permute-done
  23.7 1.0 fusion.58
  24.7 0.9 pad_dynamic-update-slice_fusion.15
  25.6 0.2 fusion.60
  25.9 1.1 fusion.63
  27.0 1.2 pad_dynamic-update-slice_fusion.14
  28.2 0.6 constant_dynamic-update-slice_fusion
  28.7 0.3 pad_dynamic-update-slice_fusion.13
  29.1 1.2 pad_dynamic-update-slice_fusion.12
  30.5 1.1 fusion.65
  31.6 8.4 %fusion.35 = (bf16[1,16,64,1024]{3,2,1,0:T(8,128)(2,1)S(1)}, f32[16,1024,64]{1,2,0:T(8,128)}) fusion(f32[64]{0:T(128)S(1)} %copy-done.6, bf16[64,576,1]{0,1,2:T(8,128)(2,1)S(1)} %bitcast.173, bf16[1,16,576,1024]{3,2,1,0:T(8,128)(2,1)S(1)} %fusion.65), kind=kOutput, calls=%fused_computation.44 | convolution fusion | flops 1218445312 | bytes 25239808 | tf_op jit(solution)/shard_map/dk,brkw->brdw/dot_general | solution.py:85
  40.0 1.3 collective-permute-start.3
  41.3 4.6 %collective-permute-start.2 = (bf16[1,1,64,1024]{3,2,1,0:T(8,128)(2,1)S(1)}, bf16[1,1,64,1024]{3,2,1,0:T(8,128)(2,1)S(1)}, u32[]{:S(2)}, u32[]{:S(2)}) collective-permute-start(bf16[1,1,64,1024]{3,2,1,0:T(8,128)(2,1)S(1)} %get-tuple-element.22), channel_id=1, source_target_pairs={{0,1},{1,2},{2,3},{3,4},{4,5},{5,6},{6,7},{8,9},{9,10},{10,11},{11... | collective-permute-start | bytes 393224 | tf_op jit(solution)/shard_map/ppermute | solution.py:15
  46.1 1.5 collective-permute-done.2
  47.7 1.0 fusion.52
  48.7 0.9 pad_dynamic-update-slice_fusion.11
  49.8 1.1 fusion.67
  50.9 1.2 pad_dynamic-update-slice_fusion.10
  52.3 0.3 pad_dynamic-update-slice_fusion.9
  52.6 1.2 pad_dynamic-update-slice_fusion.8
  54.0 1.1 fusion.69
  55.1 8.4 %convert_reduce_fusion.1 = (f32[64]{0:T(128)S(1)}, bf16[1,16,64,1024]{3,2,1,0:T(8,128)(2,1)S(1)}) fusion(bf16[1,16,64,1024]{3,2,1,0:T(8,128)(2,1)} %param.8, f32[64]{0:T(128)S(1)} %copy-done.5, bf16[64,576,1]{0,1,2:T(8,128)(2,1)S(1)} %bitcast.167, bf16[1,16,576,1024]{3,2,1,0:T(8,128)(2,1)S(1)} %fusion.69), kind=kOutput, calls=%fused_computation.47 | convolution fusion | flops 1214251008 | bytes 23142912 | tf_op jit(solution)/shard_map/dk,brkw->brdw/dot_general | solution.py:85
  63.5 12.3 %fusion.92 = f32[3,3,64,64]{3,2,1,0:T(8,128)S(1)} fusion(bf16[3,3,64,16,1024]{4,2,1,0,3:T(8,128)(2,1)} %bitcast.166, bf16[1,16,64,1024]{3,2,1,0:T(8,128)(2,1)S(1)} %get-tuple-element.38), kind=kOutput, calls=%fused_computation.128 | convolution fusion | flops 1207996416 | bytes 21118976 | tf_op jit(solution)/shard_map/brdw,brkw->dk/dot_general | solution.py:85
  76.0 4.1 %collective-permute-start.5 = (bf16[1,1,64,1024]{3,2,1,0:T(8,128)(2,1)S(1)}, bf16[1,1,64,1024]{3,2,1,0:T(8,128)(2,1)S(1)}, u32[]{:S(2)}, u32[]{:S(2)}) collective-permute-start(bf16[1,1,64,1024]{3,2,1,0:T(8,128)(2,1)S(1)} %get-tuple-element.15), channel_id=1, source_target_pairs={{0,1},{1,2},{2,3},{3,4},{4,5},{5,6},{6,7},{8,9},{9,10},{10,11},{11... | collective-permute-start | bytes 393224 | tf_op jit(solution)/shard_map/ppermute | solution.py:15
  80.0 1.7 collective-permute-start.4
  82.0 5.7 %collective-permute-done.4 = bf16[1,1,64,1024]{3,2,1,0:T(8,128)(2,1)S(1)} collective-permute-done((bf16[1,1,64,1024]{3,2,1,0:T(8,128)(2,1)S(1)}, bf16[1,1,64,1024]{3,2,1,0:T(8,128)(2,1)S(1)}, u32[]{:S(2)}, u32[]{:S(2)}) %collective-permute-start.4) | collective-permute-done | bytes 131104 | tf_op jit(solution)/shard_map/ppermute | solution.py:16
  87.6 2.4 fusion.46
  90.0 0.3 pad_dynamic-update-slice_fusion.7
  90.4 0.2 fusion.48
  90.6 1.3 fusion.71
  91.9 0.3 pad_dynamic-update-slice_fusion.6
  92.5 1.2 pad_dynamic-update-slice_fusion.5
  93.6 0.3 pad_dynamic-update-slice_fusion.4
  94.0 0.2 fusion.45
  94.2 1.3 fusion.73
  95.5 10.1 %convert_reduce_fusion = (f32[64]{0:T(128)S(1)}, bf16[1,16,64,1024]{3,2,1,0:T(8,128)(2,1)S(1)}) fusion(f32[64]{0:T(128)S(1)} %copy-done.6, f32[16,1024,64]{1,2,0:T(8,128)} %get-tuple-element.36, bf16[64,576,1]{0,1,2:T(8,128)(2,1)S(1)} %bitcast.172, bf16[1,16,576,1024]{3,2,1,0:T(8,128)(2,1)S(1)} %fusion.73), kind=kOutput, calls=%fused_computation.46 | convolution fusion | flops 1232076800 | bytes 25240064 | tf_op jit(solution)/shard_map/ck,brkw->brcw/dot_general | solution.py:85
  105.6 12.5 %fusion.101 = f32[3,3,64,64]{3,2,1,0:T(8,128)S(1)} fusion(bf16[3,3,64,16,1024]{4,2,1,0,3:T(8,128)(2,1)} %bitcast.170, bf16[1,16,64,1024]{3,2,1,0:T(8,128)(2,1)S(1)} %get-tuple-element.40), kind=kOutput, calls=%fused_computation.131 | convolution fusion | flops 1207996416 | bytes 21118976 | tf_op jit(solution)/shard_map/brdw,brkw->dk/dot_general | solution.py:85
  118.3 7.4 %collective-permute-start.7 = (bf16[1,1,64,1024]{3,2,1,0:T(8,128)(2,1)S(1)}, bf16[1,1,64,1024]{3,2,1,0:T(8,128)(2,1)S(1)}, u32[]{:S(2)}, u32[]{:S(2)}) collective-permute-start(bf16[1,1,64,1024]{3,2,1,0:T(8,128)(2,1)S(1)} %get-tuple-element.9), channel_id=1, source_target_pairs={{0,1},{1,2},{2,3},{3,4},{4,5},{5,6},{6,7},{8,9},{9,10},{10,11},{11... | collective-permute-start | bytes 393224 | tf_op jit(solution)/shard_map/ppermute | solution.py:15
  125.7 1.3 collective-permute-start.6
  127.0 4.3 %concatenate.165 = f32[73856]{0:T(1024)} concatenate(f32[36864]{0:T(1024)S(1)} %reshape.374, f32[64]{0:T(128)S(1)} %broadcast_multiply_fusion.1, f32[36864]{0:T(1024)S(1)} %reshape.376, f32[64]{0:T(128)S(1)} %broadcast_multiply_fusion), dimensions={0} | concatenate | bytes 590848 | tf_op jit(solution)/shard_map/concatenate | solution.py:89
  131.3 4.1 %collective-permute-done.6 = bf16[1,1,64,1024]{3,2,1,0:T(8,128)(2,1)S(1)} collective-permute-done((bf16[1,1,64,1024]{3,2,1,0:T(8,128)(2,1)S(1)}, bf16[1,1,64,1024]{3,2,1,0:T(8,128)(2,1)S(1)}, u32[]{:S(2)}, u32[]{:S(2)}) %collective-permute-start.6) | collective-permute-done | bytes 131104 | tf_op jit(solution)/shard_map/ppermute | solution.py:16
  135.4 2.4 fusion.40
  137.8 0.3 pad_dynamic-update-slice_fusion.3
  138.1 0.2 fusion.42
  138.4 1.3 fusion.75
  139.6 0.3 pad_dynamic-update-slice_fusion.2
  140.2 1.2 pad_dynamic-update-slice_fusion.1
  141.4 0.3 pad_dynamic-update-slice_fusion
  141.9 1.3 fusion.77
  143.2 6.7 %convert_bitcast_fusion = bf16[1,16,64,1024]{3,2,1,0:T(8,128)(2,1)} fusion(bf16[64,576,1]{0,1,2:T(8,128)(2,1)S(1)} %bitcast.169, bf16[1,16,576,1024]{3,2,1,0:T(8,128)(2,1)S(1)} %fusion.77), kind=kOutput, calls=%fused_computation.109 | convolution fusion | flops 1209008128 | bytes 21045248 | tf_op jit(solution)/shard_map/ck,brkw->brcw/dot_general | solution.py:85
  150.0 140.8 %all-reduce.26.cloned.1.call-done = f32[73856]{0:T(1024)} async-done(((f32[73856]{0:T(1024)}), f32[73856]{0:T(1024)}) %all-reduce.26.cloned.1.call-update) | async-done | bytes 295440 | tf_op jit(solution)/shard_map/psum | solution.py:90
  290.8 1.1 fusion.121
  291.9 0.8 reshape.378
  292.7 0.8 reshape.377
  293.5 1.3 fusion.120
  (40 shorter events, 2.5 us)
Async XLA Ops:
  7.2 14.8 %copy-start.2 = (bf16[3,3,64,64]{3,2,1,0:T(8,128)(2,1)S(1)}, bf16[3,3,64,64]{3,2,1,0:T(8,128)(2,1)}, u32[]{:S(2)}) copy-start(bf16[3,3,64,64]{3,2,1,0:T(8,128)(2,1)} %param.10) | copy-start | bytes 221188
  7.2 283.6 %all-reduce.26.cloned.1.call-start = ((), (), s32[]{:S(2)}) async-start(), calls=%async_computation | async-start | bytes 598016 | tf_op jit(solution)/shard_map/psum | solution.py:90
  15.8 6.9 %collective-permute-start.1 = (bf16[1,1,64,1024]{3,2,1,0:T(8,128)(2,1)S(1)}, bf16[1,1,64,1024]{3,2,1,0:T(8,128)(2,1)S(1)}, u32[]{:S(2)}, u32[]{:S(2)}) collective-permute-start(bf16[1,1,64,1024]{3,2,1,0:T(8,128)(2,1)S(1)} %get-tuple-element.27), channel_id=1, source_target_pairs={{1,0},{2,1},{3,2},{4,3},{5,4},{6,5},{7,6},{9,8},{10,9},{11,10},{12... | collective-permute-start | bytes 393224 | tf_op jit(solution)/shard_map/ppermute | solution.py:16
  17.1 6.6 %collective-permute-start = (bf16[1,1,64,1024]{3,2,1,0:T(8,128)(2,1)S(1)}, bf16[1,1,64,1024]{3,2,1,0:T(8,128)(2,1)S(1)}, u32[]{:S(2)}, u32[]{:S(2)}) collective-permute-start(bf16[1,1,64,1024]{3,2,1,0:T(8,128)(2,1)S(1)} %get-tuple-element.28), channel_id=1, source_target_pairs={{0,1},{1,2},{2,3},{3,4},{4,5},{5,6},{6,7},{8,9},{9,10},{10,11},{11... | collective-permute-start | bytes 393224 | tf_op jit(solution)/shard_map/ppermute | solution.py:15
  25.9 2.3 copy-start.1
  30.2 1.4 copy-start.6
  31.6 8.4 %copy-start.3 = (bf16[1,16,576,1024]{3,2,1,0:T(8,128)(2,1)}, bf16[1,16,576,1024]{3,2,1,0:T(8,128)(2,1)S(1)}, u32[]{:S(2)}) copy-start(bf16[1,16,576,1024]{3,2,1,0:T(8,128)(2,1)S(1)} %fusion.65) | copy-start | bytes 56623108
  31.6 14.3 %copy-start.4 = (bf16[3,3,64,64]{3,2,1,0:T(8,128)(2,1)S(1)}, bf16[3,3,64,64]{3,2,1,0:T(8,128)(2,1)}, u32[]{:S(2)}) copy-start(bf16[3,3,64,64]{3,2,1,0:T(8,128)(2,1)} %param.12) | copy-start | bytes 221188
  40.0 6.1 %collective-permute-start.3 = (bf16[1,1,64,1024]{3,2,1,0:T(8,128)(2,1)S(1)}, bf16[1,1,64,1024]{3,2,1,0:T(8,128)(2,1)S(1)}, u32[]{:S(2)}, u32[]{:S(2)}) collective-permute-start(bf16[1,1,64,1024]{3,2,1,0:T(8,128)(2,1)S(1)} %get-tuple-element.21), channel_id=1, source_target_pairs={{1,0},{2,1},{3,2},{4,3},{5,4},{6,5},{7,6},{9,8},{10,9},{11,10},{12... | collective-permute-start | bytes 393224 | tf_op jit(solution)/shard_map/ppermute | solution.py:16
  41.3 6.3 %collective-permute-start.2 = (bf16[1,1,64,1024]{3,2,1,0:T(8,128)(2,1)S(1)}, bf16[1,1,64,1024]{3,2,1,0:T(8,128)(2,1)S(1)}, u32[]{:S(2)}, u32[]{:S(2)}) collective-permute-start(bf16[1,1,64,1024]{3,2,1,0:T(8,128)(2,1)S(1)} %get-tuple-element.22), channel_id=1, source_target_pairs={{0,1},{1,2},{2,3},{3,4},{4,5},{5,6},{6,7},{8,9},{9,10},{10,11},{11... | collective-permute-start | bytes 393224 | tf_op jit(solution)/shard_map/ppermute | solution.py:15
  53.8 1.3 copy-start.5
  55.1 8.4 %copy-start = (bf16[1,16,576,1024]{3,2,1,0:T(8,128)(2,1)}, bf16[1,16,576,1024]{3,2,1,0:T(8,128)(2,1)S(1)}, u32[]{:S(2)}) copy-start(bf16[1,16,576,1024]{3,2,1,0:T(8,128)(2,1)S(1)} %fusion.69) | copy-start | bytes 56623108
  76.0 6.0 %collective-permute-start.5 = (bf16[1,1,64,1024]{3,2,1,0:T(8,128)(2,1)S(1)}, bf16[1,1,64,1024]{3,2,1,0:T(8,128)(2,1)S(1)}, u32[]{:S(2)}, u32[]{:S(2)}) collective-permute-start(bf16[1,1,64,1024]{3,2,1,0:T(8,128)(2,1)S(1)} %get-tuple-element.15), channel_id=1, source_target_pairs={{0,1},{1,2},{2,3},{3,4},{4,5},{5,6},{6,7},{8,9},{9,10},{10,11},{11... | collective-permute-start | bytes 393224 | tf_op jit(solution)/shard_map/ppermute | solution.py:15
  80.0 7.6 %collective-permute-start.4 = (bf16[1,1,64,1024]{3,2,1,0:T(8,128)(2,1)S(1)}, bf16[1,1,64,1024]{3,2,1,0:T(8,128)(2,1)S(1)}, u32[]{:S(2)}, u32[]{:S(2)}) collective-permute-start(bf16[1,1,64,1024]{3,2,1,0:T(8,128)(2,1)S(1)} %get-tuple-element.16), channel_id=1, source_target_pairs={{1,0},{2,1},{3,2},{4,3},{5,4},{6,5},{7,6},{9,8},{10,9},{11,10},{12... | collective-permute-start | bytes 393224 | tf_op jit(solution)/shard_map/ppermute | solution.py:16
  118.3 13.1 %collective-permute-start.7 = (bf16[1,1,64,1024]{3,2,1,0:T(8,128)(2,1)S(1)}, bf16[1,1,64,1024]{3,2,1,0:T(8,128)(2,1)S(1)}, u32[]{:S(2)}, u32[]{:S(2)}) collective-permute-start(bf16[1,1,64,1024]{3,2,1,0:T(8,128)(2,1)S(1)} %get-tuple-element.9), channel_id=1, source_target_pairs={{0,1},{1,2},{2,3},{3,4},{4,5},{5,6},{6,7},{8,9},{9,10},{10,11},{11... | collective-permute-start | bytes 393224 | tf_op jit(solution)/shard_map/ppermute | solution.py:15
  125.7 9.7 %collective-permute-start.6 = (bf16[1,1,64,1024]{3,2,1,0:T(8,128)(2,1)S(1)}, bf16[1,1,64,1024]{3,2,1,0:T(8,128)(2,1)S(1)}, u32[]{:S(2)}, u32[]{:S(2)}) collective-permute-start(bf16[1,1,64,1024]{3,2,1,0:T(8,128)(2,1)S(1)} %get-tuple-element.10), channel_id=1, source_target_pairs={{1,0},{2,1},{3,2},{4,3},{5,4},{6,5},{7,6},{9,8},{10,9},{11,10},{12... | collective-permute-start | bytes 393224 | tf_op jit(solution)/shard_map/ppermute | solution.py:16
Sparse Core Ops, SparseCore 0:
  131.4 159.3 all-reduce.25
where the time goes:
time: 306 us; the launch traced here: 302 us
  waiting for transfers between devices  154 us (50%)
  matrix products  58.4 us (19%)
  starting transfers between devices  26.5 us (9%)
  other arithmetic  25.8 us (8%)
  local copies, waits for them, and re-layouts  22.4 us (7%)
  between operations  14.9 us (5%)
    psum x1, waiting for transfers between devices, combine(): total = lax.psum(flat_grads, ('dp', 'space'))  141 us
    dot_general x6, matrix products, mixing(): return jnp.einsum(form, left, right, preferred_element_type=jnp.float32)  58.4 us
    ppermute x4, starting transfers between devices, extended(): before = lax.ppermute(last, axis, up)  20.9 us
    unnamed x33, local copies, waits for them, and re-layouts  12.2 us
    ppermute x4, waiting for transfers between devices, extended(): after = lax.ppermute(first, axis, down)  10.4 us
    unnamed x13, other arithmetic  7.09 us
    concatenate x4, other arithmetic, extended(): value = jnp.concatenate([before, value, after], axis=dim)  6.78 us
  transfers between devices with their start and end apart: 9, of which 7 were waited for; matrix products, arithmetic and copies ran while one was open for 6% of the time, Pallas kernels for 0%

commit v1 on v0

--- a/solution.py
+++ b/solution.py
@@ -87,7 +87,7 @@
 
 def combine(pairs):
     flat_grads = jnp.concatenate([piece.reshape(-1) for pair in pairs for piece in pair])
-    total = lax.psum(flat_grads, ("dp", "space"))
+    total = lax.psum(lax.psum(flat_grads, axis_name="space"), axis_name="dp")
     results = []
     start = 0
     for pair in pairs:

time: 306 us -> 360 us (1.18)
  waiting for transfers between devices: 154 us -> 188 us
  local copies, waits for them, and re-layouts: 22.4 us -> 29 us
  matrix products: 58.4 us -> 64.9 us
  other arithmetic: 25.8 us -> 31.5 us
    psum x1 -> x2, waiting for transfers between devices: 141 us -> 175 us  [combine(): total = lax.psum(lax.psum(flat_grads, axis_name='space'), axis_name='dp')]
    unnamed x33, local copies, waits for them, and re-layouts: 12.2 us -> 18.7 us
    dot_general x6, matrix products: 58.4 us -> 64.9 us  [mixing(): return jnp.einsum(form, left, right, preferred_element_type=jnp.float32)]
    unnamed x13, other arithmetic: 7.09 us -> 11.3 us
  transfers between devices with their start and end apart: 9 -> 10, of which waited for: 7 -> 8; matrix products, arithmetic and copies ran while one was open for 6% -> 11% of each run, Pallas kernels for 0% -> 0%
where the time goes in v1:
time: 360 us; the launch traced here: 355 us
  waiting for transfers between devices  188 us (52%)
  matrix products  64.9 us (18%)
  other arithmetic  31.5 us (9%)
  local copies, waits for them, and re-layouts  29 us (8%)
  starting transfers between devices  26.6 us (7%)
  between operations  14.8 us (4%)
    psum x2, waiting for transfers between devices, combine(): total = lax.psum(lax.psum(flat_grads, axis_name='space'), axis_name='dp')  175 us
    dot_general x6, matrix products, mixing(): return jnp.einsum(form, left, right, preferred_element_type=jnp.float32)  64.9 us
    ppermute x4, starting transfers between devices, extended(): before = lax.ppermute(last, axis, up)  20.9 us
    unnamed x33, local copies, waits for them, and re-layouts  18.7 us
    unnamed x13, other arithmetic  11.3 us
    ppermute x4, waiting for transfers between devices, extended(): after = lax.ppermute(first, axis, down)  10.3 us
  transfers between devices with their start and end apart: 10, of which 8 were waited for; matrix products, arithmetic and copies ran while one was open for 11% of the time, Pallas kernels for 0%

profile of v1, /device:TPU:1, one launch (start us, length us, event | category | flops | bytes accessed | tf_op | source)
XLA Modules:
  0.0 355.2 jit_solution(2040450000284470141)
XLA Ops:
  7.3 1.3 fusion.122
  8.6 0.6 iota_add_fusion
  9.3 0.7 add_add_fusion
  9.9 0.2 fusion.111
  10.2 3.5 fusion.106
  13.6 2.1 add_convert_fusion
  15.8 1.3 collective-permute-start.1
  17.1 4.8 %collective-permute-start = (bf16[1,1,64,1024]{3,2,1,0:T(8,128)(2,1)S(1)}, bf16[1,1,64,1024]{3,2,1,0:T(8,128)(2,1)S(1)}, u32[]{:S(2)}, u32[]{:S(2)}) collective-permute-start(bf16[1,1,64,1024]{3,2,1,0:T(8,128)(2,1)S(1)} %get-tuple-element.28), channel_id=1, source_target_pairs={{0,1},{1,2},{2,3},{3,4},{4,5},{5,6},{6,7},{8,9},{9,10},{10,11},{11... | collective-permute-start | bytes 393224 | tf_op jit(solution)/shard_map/ppermute | solution.py:15
  22.1 0.6 collective-permute-done.1
  22.7 1.0 collective-permute-done
  23.7 1.0 fusion.58
  24.7 0.9 pad_dynamic-update-slice_fusion.15
  25.9 1.1 fusion.63
  27.0 1.2 pad_dynamic-update-slice_fusion.14
  28.2 0.6 constant_dynamic-update-slice_fusion
  28.7 0.3 pad_dynamic-update-slice_fusion.13
  29.1 1.2 pad_dynamic-update-slice_fusion.12
  30.5 1.1 fusion.65
  31.6 8.4 %fusion.35 = (bf16[1,16,64,1024]{3,2,1,0:T(8,128)(2,1)S(1)}, f32[16,1024,64]{1,2,0:T(8,128)}) fusion(f32[64]{0:T(128)S(1)} %copy-done.6, bf16[64,576,1]{0,1,2:T(8,128)(2,1)S(1)} %bitcast.173, bf16[1,16,576,1024]{3,2,1,0:T(8,128)(2,1)S(1)} %fusion.65), kind=kOutput, calls=%fused_computation.44 | convolution fusion | flops 1218445312 | bytes 25239808 | tf_op jit(solution)/shard_map/dk,brkw->brdw/dot_general | solution.py:85
  40.0 1.3 collective-permute-start.3
  41.3 4.6 %collective-permute-start.2 = (bf16[1,1,64,1024]{3,2,1,0:T(8,128)(2,1)S(1)}, bf16[1,1,64,1024]{3,2,1,0:T(8,128)(2,1)S(1)}, u32[]{:S(2)}, u32[]{:S(2)}) collective-permute-start(bf16[1,1,64,1024]{3,2,1,0:T(8,128)(2,1)S(1)} %get-tuple-element.22), channel_id=1, source_target_pairs={{0,1},{1,2},{2,3},{3,4},{4,5},{5,6},{6,7},{8,9},{9,10},{10,11},{11... | collective-permute-start | bytes 393224 | tf_op jit(solution)/shard_map/ppermute | solution.py:15
  46.2 1.5 collective-permute-done.2
  47.7 1.0 fusion.52
  48.7 0.9 pad_dynamic-update-slice_fusion.11
  49.8 1.1 fusion.67
  50.9 1.2 pad_dynamic-update-slice_fusion.10
  52.3 0.3 pad_dynamic-update-slice_fusion.9
  52.6 1.2 pad_dynamic-update-slice_fusion.8
  54.0 1.1 fusion.69
  55.1 8.4 %convert_reduce_fusion.1 = (f32[64]{0:T(128)S(1)}, bf16[1,16,64,1024]{3,2,1,0:T(8,128)(2,1)S(1)}) fusion(bf16[1,16,64,1024]{3,2,1,0:T(8,128)(2,1)} %param.8, f32[64]{0:T(128)S(1)} %copy-done.5, bf16[64,576,1]{0,1,2:T(8,128)(2,1)S(1)} %bitcast.167, bf16[1,16,576,1024]{3,2,1,0:T(8,128)(2,1)S(1)} %fusion.69), kind=kOutput, calls=%fused_computation.47 | convolution fusion | flops 1214251008 | bytes 23142912 | tf_op jit(solution)/shard_map/dk,brkw->brdw/dot_general | solution.py:85
  63.5 12.3 %fusion.92 = f32[3,3,64,64]{3,2,1,0:T(8,128)S(1)} fusion(bf16[3,3,64,16,1024]{4,2,1,0,3:T(8,128)(2,1)} %bitcast.166, bf16[1,16,64,1024]{3,2,1,0:T(8,128)(2,1)S(1)} %get-tuple-element.38), kind=kOutput, calls=%fused_computation.128 | convolution fusion | flops 1207996416 | bytes 21118976 | tf_op jit(solution)/shard_map/brdw,brkw->dk/dot_general | solution.py:85
  76.0 4.1 %collective-permute-start.5 = (bf16[1,1,64,1024]{3,2,1,0:T(8,128)(2,1)S(1)}, bf16[1,1,64,1024]{3,2,1,0:T(8,128)(2,1)S(1)}, u32[]{:S(2)}, u32[]{:S(2)}) collective-permute-start(bf16[1,1,64,1024]{3,2,1,0:T(8,128)(2,1)S(1)} %get-tuple-element.15), channel_id=1, source_target_pairs={{0,1},{1,2},{2,3},{3,4},{4,5},{5,6},{6,7},{8,9},{9,10},{10,11},{11... | collective-permute-start | bytes 393224 | tf_op jit(solution)/shard_map/ppermute | solution.py:15
  80.1 1.8 collective-permute-start.4
  82.0 5.7 %collective-permute-done.4 = bf16[1,1,64,1024]{3,2,1,0:T(8,128)(2,1)S(1)} collective-permute-done((bf16[1,1,64,1024]{3,2,1,0:T(8,128)(2,1)S(1)}, bf16[1,1,64,1024]{3,2,1,0:T(8,128)(2,1)S(1)}, u32[]{:S(2)}, u32[]{:S(2)}) %collective-permute-start.4) | collective-permute-done | bytes 131104 | tf_op jit(solution)/shard_map/ppermute | solution.py:16
  87.6 2.4 fusion.46
  90.0 0.3 pad_dynamic-update-slice_fusion.7
  90.6 1.3 fusion.71
  91.9 0.3 pad_dynamic-update-slice_fusion.6
  92.5 1.2 pad_dynamic-update-slice_fusion.5
  93.6 0.3 pad_dynamic-update-slice_fusion.4
  94.2 1.3 fusion.73
  95.5 10.1 %convert_reduce_fusion = (f32[64]{0:T(128)S(1)}, bf16[1,16,64,1024]{3,2,1,0:T(8,128)(2,1)S(1)}) fusion(f32[64]{0:T(128)S(1)} %copy-done.6, f32[16,1024,64]{1,2,0:T(8,128)} %get-tuple-element.36, bf16[64,576,1]{0,1,2:T(8,128)(2,1)S(1)} %bitcast.172, bf16[1,16,576,1024]{3,2,1,0:T(8,128)(2,1)S(1)} %fusion.73), kind=kOutput, calls=%fused_computation.46 | convolution fusion | flops 1232076800 | bytes 25240064 | tf_op jit(solution)/shard_map/ck,brkw->brcw/dot_general | solution.py:85
  105.7 12.3 %fusion.101 = f32[3,3,64,64]{3,2,1,0:T(8,128)S(1)} fusion(bf16[3,3,64,16,1024]{4,2,1,0,3:T(8,128)(2,1)} %bitcast.170, bf16[1,16,64,1024]{3,2,1,0:T(8,128)(2,1)S(1)} %get-tuple-element.40), kind=kOutput, calls=%fused_computation.131 | convolution fusion | flops 1207996416 | bytes 21118976 | tf_op jit(solution)/shard_map/brdw,brkw->dk/dot_general | solution.py:85
  118.1 7.4 %collective-permute-start.7 = (bf16[1,1,64,1024]{3,2,1,0:T(8,128)(2,1)S(1)}, bf16[1,1,64,1024]{3,2,1,0:T(8,128)(2,1)S(1)}, u32[]{:S(2)}, u32[]{:S(2)}) collective-permute-start(bf16[1,1,64,1024]{3,2,1,0:T(8,128)(2,1)S(1)} %get-tuple-element.9), channel_id=1, source_target_pairs={{0,1},{1,2},{2,3},{3,4},{4,5},{5,6},{6,7},{8,9},{9,10},{10,11},{11... | collective-permute-start | bytes 393224 | tf_op jit(solution)/shard_map/ppermute | solution.py:15
  125.5 1.3 collective-permute-start.6
  126.8 4.4 %concatenate.165 = f32[73856]{0:T(1024)} concatenate(f32[36864]{0:T(1024)S(1)} %reshape.374, f32[64]{0:T(128)S(1)} %broadcast_multiply_fusion.1, f32[36864]{0:T(1024)S(1)} %reshape.376, f32[64]{0:T(128)S(1)} %broadcast_multiply_fusion), dimensions={0} | concatenate | bytes 590848 | tf_op jit(solution)/shard_map/concatenate | solution.py:89
  131.3 4.0 %collective-permute-done.6 = bf16[1,1,64,1024]{3,2,1,0:T(8,128)(2,1)S(1)} collective-permute-done((bf16[1,1,64,1024]{3,2,1,0:T(8,128)(2,1)S(1)}, bf16[1,1,64,1024]{3,2,1,0:T(8,128)(2,1)S(1)}, u32[]{:S(2)}, u32[]{:S(2)}) %collective-permute-start.6) | collective-permute-done | bytes 131104 | tf_op jit(solution)/shard_map/ppermute | solution.py:16
  135.2 2.5 fusion.40
  137.8 1.6 pad_dynamic-update-slice_fusion.3
  139.4 1.6 fusion.42
  141.0 2.7 fusion.75
  143.7 1.7 pad_dynamic-update-slice_fusion.2
  145.4 1.6 constant_dynamic-update-slice_fusion.3
  147.0 2.5 pad_dynamic-update-slice_fusion.1
  149.4 1.6 pad_dynamic-update-slice_fusion
  151.1 1.6 fusion.39
  152.7 2.6 fusion.77
  155.3 70.4 %all-reduce.27.cloned.1.call-done = f32[73856]{0:T(1024)} async-done(((f32[73856]{0:T(1024)}), f32[73856]{0:T(1024)}) %all-reduce.27.cloned.1.call-update) | async-done | bytes 295440 | tf_op jit(solution)/shard_map/psum | solution.py:90
  225.7 13.5 %convert_bitcast_fusion = bf16[1,16,64,1024]{3,2,1,0:T(8,128)(2,1)} fusion(bf16[64,576,1]{0,1,2:T(8,128)(2,1)S(1)} %bitcast.169, bf16[1,16,576,1024]{3,2,1,0:T(8,128)(2,1)} %fusion.77), kind=kOutput, calls=%fused_computation.109 | convolution fusion | flops 1209008128 | bytes 21045248 | tf_op jit(solution)/shard_map/ck,brkw->brcw/dot_general | solution.py:85
  239.2 105.0 %all-reduce.29.cloned.1.call-done = f32[73856]{0:T(1024)} async-done(((f32[73856]{0:T(1024)}), f32[73856]{0:T(1024)}) %all-reduce.29.cloned.1.call-update) | async-done | bytes 295440 | tf_op jit(solution)/shard_map/psum | solution.py:90
  344.1 1.1 fusion.121
  345.2 0.8 reshape.378
  346.1 0.8 reshape.377
  346.9 1.3 fusion.120
  (43 shorter events, 2.7 us)
Async XLA Ops:
  7.2 14.8 %copy-start.2 = (bf16[3,3,64,64]{3,2,1,0:T(8,128)(2,1)S(1)}, bf16[3,3,64,64]{3,2,1,0:T(8,128)(2,1)}, u32[]{:S(2)}) copy-start(bf16[3,3,64,64]{3,2,1,0:T(8,128)(2,1)} %param.10) | copy-start | bytes 221188
  7.2 218.5 %all-reduce.27.cloned.1.call-start = ((), (), s32[]{:S(2)}) async-start(), calls=%async_computation | async-start | bytes 598016 | tf_op jit(solution)/shard_map/psum | solution.py:90
  15.8 6.9 %collective-permute-start.1 = (bf16[1,1,64,1024]{3,2,1,0:T(8,128)(2,1)S(1)}, bf16[1,1,64,1024]{3,2,1,0:T(8,128)(2,1)S(1)}, u32[]{:S(2)}, u32[]{:S(2)}) collective-permute-start(bf16[1,1,64,1024]{3,2,1,0:T(8,128)(2,1)S(1)} %get-tuple-element.27), channel_id=1, source_target_pairs={{1,0},{2,1},{3,2},{4,3},{5,4},{6,5},{7,6},{9,8},{10,9},{11,10},{12... | collective-permute-start | bytes 393224 | tf_op jit(solution)/shard_map/ppermute | solution.py:16
  17.1 6.6 %collective-permute-start = (bf16[1,1,64,1024]{3,2,1,0:T(8,128)(2,1)S(1)}, bf16[1,1,64,1024]{3,2,1,0:T(8,128)(2,1)S(1)}, u32[]{:S(2)}, u32[]{:S(2)}) collective-permute-start(bf16[1,1,64,1024]{3,2,1,0:T(8,128)(2,1)S(1)} %get-tuple-element.28), channel_id=1, source_target_pairs={{0,1},{1,2},{2,3},{3,4},{4,5},{5,6},{6,7},{8,9},{9,10},{10,11},{11... | collective-permute-start | bytes 393224 | tf_op jit(solution)/shard_map/ppermute | solution.py:15
  25.9 2.3 copy-start.1
  30.2 1.4 copy-start.6
  31.6 8.4 %copy-start.3 = (bf16[1,16,576,1024]{3,2,1,0:T(8,128)(2,1)}, bf16[1,16,576,1024]{3,2,1,0:T(8,128)(2,1)S(1)}, u32[]{:S(2)}) copy-start(bf16[1,16,576,1024]{3,2,1,0:T(8,128)(2,1)S(1)} %fusion.65) | copy-start | bytes 56623108
  31.6 14.3 %copy-start.4 = (bf16[3,3,64,64]{3,2,1,0:T(8,128)(2,1)S(1)}, bf16[3,3,64,64]{3,2,1,0:T(8,128)(2,1)}, u32[]{:S(2)}) copy-start(bf16[3,3,64,64]{3,2,1,0:T(8,128)(2,1)} %param.12) | copy-start | bytes 221188
  40.0 6.1 %collective-permute-start.3 = (bf16[1,1,64,1024]{3,2,1,0:T(8,128)(2,1)S(1)}, bf16[1,1,64,1024]{3,2,1,0:T(8,128)(2,1)S(1)}, u32[]{:S(2)}, u32[]{:S(2)}) collective-permute-start(bf16[1,1,64,1024]{3,2,1,0:T(8,128)(2,1)S(1)} %get-tuple-element.21), channel_id=1, source_target_pairs={{1,0},{2,1},{3,2},{4,3},{5,4},{6,5},{7,6},{9,8},{10,9},{11,10},{12... | collective-permute-start | bytes 393224 | tf_op jit(solution)/shard_map/ppermute | solution.py:16
  41.3 6.4 %collective-permute-start.2 = (bf16[1,1,64,1024]{3,2,1,0:T(8,128)(2,1)S(1)}, bf16[1,1,64,1024]{3,2,1,0:T(8,128)(2,1)S(1)}, u32[]{:S(2)}, u32[]{:S(2)}) collective-permute-start(bf16[1,1,64,1024]{3,2,1,0:T(8,128)(2,1)S(1)} %get-tuple-element.22), channel_id=1, source_target_pairs={{0,1},{1,2},{2,3},{3,4},{4,5},{5,6},{6,7},{8,9},{9,10},{10,11},{11... | collective-permute-start | bytes 393224 | tf_op jit(solution)/shard_map/ppermute | solution.py:15
  53.8 1.3 copy-start.5
  55.1 8.4 %copy-start = (bf16[1,16,576,1024]{3,2,1,0:T(8,128)(2,1)}, bf16[1,16,576,1024]{3,2,1,0:T(8,128)(2,1)S(1)}, u32[]{:S(2)}) copy-start(bf16[1,16,576,1024]{3,2,1,0:T(8,128)(2,1)S(1)} %fusion.69) | copy-start | bytes 56623108
  76.0 6.0 %collective-permute-start.5 = (bf16[1,1,64,1024]{3,2,1,0:T(8,128)(2,1)S(1)}, bf16[1,1,64,1024]{3,2,1,0:T(8,128)(2,1)S(1)}, u32[]{:S(2)}, u32[]{:S(2)}) collective-permute-start(bf16[1,1,64,1024]{3,2,1,0:T(8,128)(2,1)S(1)} %get-tuple-element.15), channel_id=1, source_target_pairs={{0,1},{1,2},{2,3},{3,4},{4,5},{5,6},{6,7},{8,9},{9,10},{10,11},{11... | collective-permute-start | bytes 393224 | tf_op jit(solution)/shard_map/ppermute | solution.py:15
  80.1 7.6 %collective-permute-start.4 = (bf16[1,1,64,1024]{3,2,1,0:T(8,128)(2,1)S(1)}, bf16[1,1,64,1024]{3,2,1,0:T(8,128)(2,1)S(1)}, u32[]{:S(2)}, u32[]{:S(2)}) collective-permute-start(bf16[1,1,64,1024]{3,2,1,0:T(8,128)(2,1)S(1)} %get-tuple-element.16), channel_id=1, source_target_pairs={{1,0},{2,1},{3,2},{4,3},{5,4},{6,5},{7,6},{9,8},{10,9},{11,10},{12... | collective-permute-start | bytes 393224 | tf_op jit(solution)/shard_map/ppermute | solution.py:16
  118.1 13.2 %collective-permute-start.7 = (bf16[1,1,64,1024]{3,2,1,0:T(8,128)(2,1)S(1)}, bf16[1,1,64,1024]{3,2,1,0:T(8,128)(2,1)S(1)}, u32[]{:S(2)}, u32[]{:S(2)}) collective-permute-start(bf16[1,1,64,1024]{3,2,1,0:T(8,128)(2,1)S(1)} %get-tuple-element.9), channel_id=1, source_target_pairs={{0,1},{1,2},{2,3},{3,4},{4,5},{5,6},{6,7},{8,9},{9,10},{10,11},{11... | collective-permute-start | bytes 393224 | tf_op jit(solution)/shard_map/ppermute | solution.py:15
  125.5 9.7 %collective-permute-start.6 = (bf16[1,1,64,1024]{3,2,1,0:T(8,128)(2,1)S(1)}, bf16[1,1,64,1024]{3,2,1,0:T(8,128)(2,1)S(1)}, u32[]{:S(2)}, u32[]{:S(2)}) collective-permute-start(bf16[1,1,64,1024]{3,2,1,0:T(8,128)(2,1)S(1)} %get-tuple-element.10), channel_id=1, source_target_pairs={{1,0},{2,1},{3,2},{4,3},{5,4},{6,5},{7,6},{9,8},{10,9},{11,10},{12... | collective-permute-start | bytes 393224 | tf_op jit(solution)/shard_map/ppermute | solution.py:16
  131.2 213.0 %all-reduce.29.cloned.1.call-start = ((), (), s32[]{:S(2)}) async-start(), calls=%async_computation.1 | async-start | bytes 598016 | tf_op jit(solution)/shard_map/psum | solution.py:90
Sparse Core Ops, SparseCore 0:
  131.3 94.3 all-reduce.26
  228.2 115.9 all-reduce.28
